TPU v7x, 32 devices: a whole 2x2x4 slice. The times are simulated.
32 devices in a mesh: site: 4 (over z), bond: 8 (over y, x, core).
Axes of the slice: x: 2, y: 2, z: 4, core: 2. Of those that a mesh axis runs over, the one named last changes fastest.
Arguments:
- site_tensor: float32 [4, 4, 3072, 3072], P('site', None, 'bond'), may hold values from -0.15625 to 0.15625
- panels: float32 [4, 3072, 128], P('site', 'bond'), may hold values from -6 to 6
- fresh: float32 [1, 3072, 128], P(None, 'bond'), may hold values from -6 to 6
- outcomes: int32 [4, 2, 128], P('site'), may hold values from 0 to 3, as said below
Outputs:
- carried: float32 [4, 2, 3072, 128], P('site', None, 'bond')
Inputs may be any that keep to these rules, and one draw needn't show every extreme that they name: `outcomes`: at each site and tick, every outcome is taken by at most 48 samples, and some outcome by exactly 48.
All inputs are finite; a program needn't handle non-finite values.
Results may differ from a plain program's by a relative error of at most 0.0001.
Values sent between devices are 32-bit elements; how exact they have to be, the bound alone decides.
A program may use at most 64 MiB of HBM per device.

v0:
```python
import jax
import jax.numpy as jnp
from jax import lax
from jax.sharding import PartitionSpec as P

TICKS = 2


def from_behind(value, axis, steps):
    count = lax.axis_size(axis)
    initial, last = (max(0, -steps), min(count, count - steps))
    return lax.ppermute(value, axis, [(source, source + steps) for source in range(initial, last)])


def contribute(tensor, vectors, selected):
    outcome_count = tensor.shape[0]
    chosen = (selected[None, :] == jnp.arange(outcome_count, dtype=jnp.int32)[:, None]).astype(
        jnp.float32
    )
    products = lax.dot_general(
        tensor,
        vectors,
        (((1,), (0,)), ((), ())),
        precision=lax.Precision.HIGHEST,
        preferred_element_type=jnp.float32,
    )
    return jnp.sum(products * chosen[:, None, :], axis=0)


def advance(tensor, vectors, selected):
    return lax.psum_scatter(
        contribute(tensor, vectors, selected), "bond", scatter_dimension=0, tiled=True
    )


def on_device(site_tensor, panels, fresh, outcomes):
    tensor = site_tensor[0]
    current = panels[0]
    results = []
    for tick_index in range(TICKS):
        produced = advance(tensor, current, outcomes[0, tick_index])
        results.append(produced)
        if tick_index + 1 < TICKS:
            passed = from_behind(produced, "site", 1)
            current = jnp.where(lax.axis_index("site") == 0, fresh[tick_index], passed)
    return jnp.stack(results, 0)[None]


def solution(mesh):
    placed = (
        P("site", None, "bond", None),
        P("site", "bond", None),
        P(None, "bond", None),
        P("site", None, None),
    )
    return jax.shard_map(
        on_device,
        mesh=mesh,
        in_specs=placed,
        out_specs=P("site", None, "bond", None),
        check_vma=False,
    )
```

profile of v0, /device:TPU:8, one launch (start us, length us, event | category | flops | bytes accessed | tf_op | source)
XLA Modules:
  0.0 155.7 jit_solution(10290321736743150412)
XLA Ops:
  6.5 0.0 copy-start
  6.5 0.0 reduce-scatter.3.cloned.1.call-start
  6.5 0.8 slice_bitcast_fusion.1
  7.3 0.2 copy-done
  7.5 0.0 copy-start.1
  7.5 34.0 %multiply_reduce_fusion = f32[3072,128]{1,0:T(8,128)} fusion(f32[1,4,384,3072]{3,2,1,0:T(8,128)} %param.4, f32[4,128]{1,0:T(4,128)S(1)} %fusion.12, f32[1,384,128]{2,1,0:T(8,128)S(1)} %copy-done), kind=kOutput, calls=%fused_computation.6 | convolution fusion | flops 7250509824 | bytes 20645888 | tf_op jit(solution)/shard_map/dot_general | solution.py:20
  41.5 0.0 reduce-scatter.3.cloned.1.call-update
  41.5 0.0 reduce-scatter.5.cloned.1.call-start
  41.5 39.6 %reduce-scatter.3.cloned.1.call-done = f32[384,128]{1,0:T(8,128)} async-done(((f32[3072,128]{1,0:T(8,128)}), f32[384,128]{1,0:T(8,128)}) %reduce-scatter.3.cloned.1.call-update) | async-done | bytes 196624 | tf_op jit(solution)/shard_map/reduce_scatter | solution.py:31
  81.1 3.6 %collective-permute-start = (f32[384,128]{1,0:T(8,128)}, f32[384,128]{1,0:T(8,128)S(1)}, u32[]{:S(2)}, u32[]{:S(2)}) collective-permute-start(f32[384,128]{1,0:T(8,128)} %reduce-scatter.3.cloned.1.call-done), channel_id=1, source_target_pairs={{0,8},{8,16},{16,24},{1,9},{9,17},{17,25},{2,10},{10,18},{18,26},{... | collective-permute-start | bytes 589832 | tf_op jit(solution)/shard_map/ppermute | solution.py:12
  84.7 0.0 copy-start.2
  84.7 4.9 %collective-permute-done = f32[384,128]{1,0:T(8,128)S(1)} collective-permute-done((f32[384,128]{1,0:T(8,128)}, f32[384,128]{1,0:T(8,128)S(1)}, u32[]{:S(2)}, u32[]{:S(2)}) %collective-permute-start) | collective-permute-done | bytes 196640 | tf_op jit(solution)/shard_map/ppermute | solution.py:12
  89.6 0.0 copy-done.1
  89.6 17.4 %fusion.4 = f32[3072,128]{0,1:T(8,128)S(1)} fusion(f32[1,4,384,3072]{3,2,1,0:T(8,128)} %param.4, f32[4,128]{1,0:T(4,128)S(1)} %fusion.13, f32[384,128]{1,0:T(8,128)S(1)} %collective-permute-done, f32[1,384,128]{2,1,0:T(8,128)S(1)} %copy-done.1, pred[]{:T(512)S(6)} %eq.45), kind=kOutput, calls=%fused_computation.5 | convolution fusion | flops 7250558976 | bytes 20842496 | tf_op jit(solution)/shard_map/dot_general | solution.py:20
  107.0 1.6 %copy.12 = f32[3072,128]{1,0:T(8,128)} copy(f32[3072,128]{0,1:T(8,128)S(1)} %fusion.4) | data formatting | bytes 3145728 | tf_op jit(solution)/shard_map/reduce_sum | solution.py:27
  108.6 0.0 reduce-scatter.5.cloned.1.call-update
  108.7 38.5 %reduce-scatter.5.cloned.1.call-done = f32[384,128]{1,0:T(8,128)} async-done(((f32[3072,128]{1,0:T(8,128)}), f32[384,128]{1,0:T(8,128)}) %reduce-scatter.5.cloned.1.call-update) | async-done | bytes 196624 | tf_op jit(solution)/shard_map/reduce_scatter | solution.py:31
  147.1 0.0 copy-done.2
  147.1 1.7 %maximum_bitcast_fusion = f32[1,2,384,128]{3,2,1,0:T(8,128)} fusion(f32[1,384,128]{2,1,0:T(8,128)} %bitcast.34, f32[1,384,128]{2,1,0:T(8,128)S(1)} %bitcast.33), kind=kLoop, calls=%fused_computation.7 | loop fusion | flops 98304 | bytes 786432 | tf_op jit(solution)/shard_map/broadcast_in_dim | solution.py:46
  (2 shorter events, 0.0 us)
Async XLA Ops:
  6.5 1.0 copy-start
  6.5 74.6 %reduce-scatter.3.cloned.1.call-start = ((), (), s32[]{:S(2)}) async-start(), calls=%async_computation.2 | async-start | bytes 1769472 | tf_op jit(solution)/shard_map/reduce_scatter | solution.py:31
  7.5 82.2 %copy-start.1 = (f32[1,384,128]{2,1,0:T(8,128)S(1)}, f32[1,384,128]{2,1,0:T(8,128)}, u32[]{:S(2)}) copy-start(f32[1,384,128]{2,1,0:T(8,128)} %param.6) | copy-start | bytes 589828
  41.5 105.7 %reduce-scatter.5.cloned.1.call-start = ((), (), s32[]{:S(2)}) async-start(), calls=%async_computation.3 | async-start | bytes 1769472 | tf_op jit(solution)/shard_map/reduce_scatter | solution.py:31
  81.1 8.5 %collective-permute-start = (f32[384,128]{1,0:T(8,128)}, f32[384,128]{1,0:T(8,128)S(1)}, u32[]{:S(2)}, u32[]{:S(2)}) collective-permute-start(f32[384,128]{1,0:T(8,128)} %reduce-scatter.3.cloned.1.call-done), channel_id=1, source_target_pairs={{0,8},{8,16},{16,24},{1,9},{9,17},{17,25},{2,10},{10,18},{18,26},{... | collective-permute-start | bytes 589832 | tf_op jit(solution)/shard_map/ppermute | solution.py:12
  84.7 62.4 %copy-start.2 = (f32[384,128]{1,0:T(8,128)S(1)}, f32[384,128]{1,0:T(8,128)}, u32[]{:S(2)}) copy-start(f32[384,128]{1,0:T(8,128)} %reduce-scatter.3.cloned.1.call-done) | copy-start | bytes 589828
Sparse Core Ops, SparseCore 0:
  41.6 39.4 reduce-scatter.2
  108.8 38.3 reduce-scatter.4
where the time goes:
time: 157 us; the launch traced here: 156 us
  waiting for transfers between devices  83 us (53%)
  matrix products  51.3 us (33%)
  between operations  13.4 us (9%)
  starting transfers between devices  3.62 us (2%)
  local copies, waits for them, and re-layouts  2.58 us (2%)
  other arithmetic  1.71 us (1%)
    reduce_scatter x2, waiting for transfers between devices, advance(): lax.psum_scatter(contribute(tensor, vectors, selected), 'bond', scatter_d...  78 us
    dot_general x2, matrix products, contribute(): lax.dot_general(tensor, vectors, (((1,), (0,)), ((), ())), precision=lax....  51.3 us
    ppermute x1, waiting for transfers between devices, from_behind(): lax.ppermute(value, axis, [(source, source + steps) for source in range(i...  4.94 us
    ppermute x1, starting transfers between devices, from_behind(): lax.ppermute(value, axis, [(source, source + steps) for source in range(i...  3.57 us
  transfers between devices with their start and end apart: 3, of which 3 were waited for; matrix products, arithmetic and copies ran while one was open for 0% of the time, Pallas kernels for 0%

commit v1 on v0

v1 whole, which is shorter than its diff:
```python
import functools
import math

import jax
import jax.numpy as jnp
from jax import lax
from jax.experimental import pallas as pl
from jax.experimental.pallas import tpu as pltpu
from jax.sharding import PartitionSpec as P

TILE = 256


def flipped(index, mask):
    result = index
    bit = 0
    while (1 << bit) <= mask:
        if mask >> bit & 1:
            result = result + (1 - 2 * ((index // (1 << bit)) % 2)) * (1 << bit)
        bit += 1
    return result


def kernel(
    plan,
    tensor_ref,
    panel_ref,
    fresh_ref,
    outcome_ref,
    out_ref,
    raw,
    high,
    low,
    stacked,
    left,
    part,
    core_in,
    stage_in,
    hop_in,
    load_sem,
    core_send,
    core_recv,
    stage_send,
    stage_recv,
    hop_send,
    hop_recv,
):
    sites, bond, ticks, count, rows, samples, chunk, width = plan
    bits = bond.bit_length() - 1
    uppers = 1 << (bits - 1)
    per_block = width // chunk
    blocks = bond // per_block
    tiles = width // TILE
    half = chunk // 2
    orders = (tuple(range(1, bits)), tuple(reversed(range(1, bits))))

    me = lax.axis_index("bond")
    site = lax.axis_index("site")

    def at(bond_mask):
        return {"bond": flipped(me, bond_mask)}

    def load(step, tile):
        block = flipped(me // per_block, blocks - 1 - step)
        column = pl.multiple_of(block * width + tile * TILE, TILE)
        return pltpu.make_async_copy(
            tensor_ref.at[0, :, :, pl.ds(column, TILE)],
            raw.at[step * tiles + tile],
            load_sem.at[step * tiles + tile],
        )

    for step in range(blocks):
        for tile in range(tiles):
            load(step, tile).start()

    barrier = pltpu.get_barrier_semaphore()
    for bit in range(bits):
        pl.semaphore_signal(
            barrier, inc=1, device_id=at(1 << bit), device_id_type=pl.DeviceIdType.MESH
        )

    @pl.when(site > 0)
    def _():
        pl.semaphore_signal(
            barrier, inc=1, device_id={"site": site - 1}, device_id_type=pl.DeviceIdType.MESH
        )

    @pl.when(site < sites - 1)
    def _():
        pl.semaphore_signal(
            barrier, inc=1, device_id={"site": site + 1}, device_id_type=pl.DeviceIdType.MESH
        )

    def prepare(vectors, tick):
        chosen = outcome_ref[0, pl.ds(tick, 1), :]
        for outcome in range(count):
            stacked[pl.ds(outcome * rows, rows), :] = jnp.where(chosen == outcome, vectors, 0.0)
        turned = stacked[...].T
        upper = turned.astype(jnp.bfloat16)
        left[pl.ds(0, samples), :] = upper
        left[pl.ds(samples, samples), :] = (turned - upper.astype(jnp.float32)).astype(jnp.bfloat16)

    def compute(tick, step):
        def one(tile):
            index = step * tiles + tile
            if tick == 0:
                load(step, tile).wait()
                for outcome in range(count):
                    values = raw[index, outcome]
                    upper = values.astype(jnp.bfloat16)
                    high[index, pl.ds(outcome * rows, rows), :] = upper
                    low[index, pl.ds(outcome * rows, rows), :] = (
                        values - upper.astype(jnp.float32)
                    ).astype(jnp.bfloat16)
            both = jnp.dot(left[...], high[index], preferred_element_type=jnp.float32)
            rest = jnp.dot(
                left[pl.ds(0, samples), :], low[index], preferred_element_type=jnp.float32
            )
            total = both[:samples] + (both[samples:] + rest)
            part[tick, step, pl.ds(pl.multiple_of(tile * TILE, TILE), TILE), :] = total.T

        if plan_unroll:
            for tile in range(tiles):
                one(tile)
        else:
            lax.fori_loop(0, tiles, lambda tile, _: (one(tile), 0)[1], 0)

    plan_unroll = True

    def place(rel):
        step = blocks - 1 - rel // per_block
        offset = flipped(me % per_block, rel % per_block) * chunk
        return step, offset

    def rows_of(tick, rel, start, size):
        step, offset = place(rel)
        return part.at[tick, step, pl.ds(pl.multiple_of(offset + start, 8), size), :]

    def core_copy(tick, upper):
        return pltpu.make_async_remote_copy(
            src_ref=rows_of(tick, 2 * upper + 1, 0, chunk),
            dst_ref=core_in.at[tick, upper],
            send_sem=core_send.at[tick, upper],
            recv_sem=core_recv.at[tick, upper],
            device_id=at(1),
            device_id_type=pl.DeviceIdType.MESH,
        )

    def first_bit(upper, side):
        for position, bit in enumerate(orders[side]):
            if upper >> (bit - 1) & 1:
                return position, bit
        return len(orders[side]), None

    def stage_copy(tick, upper, side):
        _, bit = first_bit(upper, side)
        return pltpu.make_async_remote_copy(
            src_ref=rows_of(tick, 2 * upper, side * half, half),
            dst_ref=stage_in.at[tick, upper - 1, side],
            send_sem=stage_send.at[tick, upper - 1, side],
            recv_sem=stage_recv.at[tick, upper - 1, side],
            device_id=at(1 << bit),
            device_id_type=pl.DeviceIdType.MESH,
        )

    def hop_copy(side):
        return pltpu.make_async_remote_copy(
            src_ref=out_ref.at[0, 0, pl.ds(side * half, half), :],
            dst_ref=hop_in.at[pl.ds(side * half, half), :],
            send_sem=hop_send.at[side],
            recv_sem=hop_recv.at[side],
            device_id={"site": site + 1},
            device_id_type=pl.DeviceIdType.MESH,
        )

    def settle(tick, upper):
        core_copy(tick, upper).wait_recv()
        sides = sorted(range(2), key=lambda side: first_bit(upper, side)[0])
        for side in sides:
            position, bit = first_bit(upper, side)
            own = rows_of(tick, 2 * upper, side * half, half)
            total = own[...] + core_in[tick, upper, pl.ds(side * half, half), :]
            for earlier in orders[side][:position]:
                source = upper | 1 << (earlier - 1)
                stage_copy(tick, source, side).wait_recv()
                total = total + stage_in[tick, source - 1, side]
            if bit is None:
                out_ref[0, tick, pl.ds(side * half, half), :] = total
                if tick == 0:

                    @pl.when(site < sites - 1)
                    def _():
                        hop_copy(side).start()

            else:
                own[...] = total
                stage_copy(tick, upper, side).start()

    def greet():
        edges = (site > 0).astype(jnp.int32) + (site < sites - 1).astype(jnp.int32)
        pl.semaphore_wait(barrier, bits + edges)

    for tick in range(ticks):
        if tick == 0:
            prepare(panel_ref[0], 0)
        else:

            @pl.when(site == 0)
            def _():
                hop_in[...] = fresh_ref[tick - 1]

            @pl.when(site > 0)
            def _():
                for side in range(2):
                    hop_copy(side).wait_recv()

            prepare(hop_in[...], tick)
        group = per_block // 2
        pending = []
        for step in range(blocks):
            compute(tick, step)
            if tick == 0 and step == 0:
                greet()
            block = blocks - 1 - step
            ready = [block * group + inner for inner in reversed(range(group))]
            for upper in ready:
                core_copy(tick, upper).start()
            for upper in pending:
                settle(tick, upper)
            pending = ready
        for upper in pending:
            settle(tick, upper)

    for tick in range(ticks):
        for upper in range(uppers):
            core_copy(tick, upper).wait_send()
            if upper:
                for side in range(2):
                    stage_copy(tick, upper, side).wait_send()

    @pl.when(site < sites - 1)
    def _():
        for side in range(2):
            hop_copy(side).wait_send()


def on_device(sites, bond, site_tensor, panels, fresh, outcomes):
    _, count, rows, columns = site_tensor.shape
    samples = panels.shape[2]
    ticks = outcomes.shape[1]
    chunk = columns // bond
    width = math.lcm(TILE, 2 * chunk)
    blocks = columns // width
    tiles = columns // TILE
    depth = count * rows
    uppers = bond // 2
    half = chunk // 2
    plan = (sites, bond, ticks, count, rows, samples, chunk, width)
    dma = pltpu.SemaphoreType.DMA
    return pl.pallas_call(
        functools.partial(kernel, plan),
        out_shape=jax.ShapeDtypeStruct((1, ticks, chunk, samples), jnp.float32),
        in_specs=[pl.BlockSpec(memory_space=pl.ANY)]
        + [pl.BlockSpec(memory_space=pltpu.VMEM)] * 3,
        out_specs=pl.BlockSpec(memory_space=pltpu.VMEM),
        scratch_shapes=[
            pltpu.VMEM((tiles, count, rows, TILE), jnp.float32),
            pltpu.VMEM((tiles, depth, TILE), jnp.bfloat16),
            pltpu.VMEM((tiles, depth, TILE), jnp.bfloat16),
            pltpu.VMEM((depth, samples), jnp.float32),
            pltpu.VMEM((2 * samples, depth), jnp.bfloat16),
            pltpu.VMEM((ticks, blocks, width, samples), jnp.float32),
            pltpu.VMEM((ticks, uppers, chunk, samples), jnp.float32),
            pltpu.VMEM((ticks, uppers - 1, 2, half, samples), jnp.float32),
            pltpu.VMEM((chunk, samples), jnp.float32),
            dma((tiles,)),
            dma((ticks, uppers)),
            dma((ticks, uppers)),
            dma((ticks, uppers - 1, 2)),
            dma((ticks, uppers - 1, 2)),
            dma((2,)),
            dma((2,)),
        ],
        compiler_params=pltpu.CompilerParams(
            collective_id=0, has_side_effects=True, vmem_limit_bytes=60 * 1024 * 1024
        ),
        name="window",
    )(site_tensor, panels, fresh, outcomes)


def solution(mesh):
    placed = (
        P("site", None, "bond", None),
        P("site", "bond", None),
        P(None, "bond", None),
        P("site", None, None),
    )
    return jax.shard_map(
        functools.partial(on_device, mesh.shape["site"], mesh.shape["bond"]),
        mesh=mesh,
        in_specs=placed,
        out_specs=P("site", None, "bond", None),
        check_vma=False,
    )
```

time: 157 us -> 39.8 us (0.25)
  waiting for transfers between devices: 83 us -> 0 us
  matrix products: 51.3 us -> 0 us
  Pallas kernels: 0 us -> 37.8 us
  between operations: 13.4 us -> 0.01 us
  starting transfers between devices: 3.62 us -> 0 us
  other arithmetic: 1.71 us -> 0 us
    reduce_scatter x2 -> x0, waiting for transfers between devices: 78 us -> none  [advance(): lax.psum_scatter(contribute(tensor, vectors, selected), 'bond', scatter_d...]
    dot_general x2 -> x0, matrix products: 51.3 us -> none  [contribute(): lax.dot_general(tensor, vectors, (((1,), (0,)), ((), ())), precision=lax....]
    pallas_call x0 -> x1, Pallas kernels: none -> 37.8 us  [on_device(): pl.pallas_call(functools.partial(kernel, plan), out_shape=jax.ShapeDtypeS...]
    ppermute x1 -> x0, waiting for transfers between devices: 4.94 us -> none  [from_behind(): lax.ppermute(value, axis, [(source, source + steps) for source in range(i...]
    ppermute x1 -> x0, starting transfers between devices: 3.57 us -> none  [from_behind(): lax.ppermute(value, axis, [(source, source + steps) for source in range(i...]
    broadcast_in_dim x1 -> x0, other arithmetic: 1.7 us -> none  [on_device(): return jnp.stack(results, 0)[None]]
    reduce_sum x1 -> x0, local copies, waits for them, and re-layouts: 1.63 us -> none  [contribute(): return jnp.sum(products * chosen[:, None, :], axis=0)]
  transfers between devices with their start and end apart: 3 -> 0, of which waited for: 3 -> 0; matrix products, arithmetic and copies ran while one was open for 0% -> 0% of each run, Pallas kernels for 0% -> 0%
where the time goes in v1:
time: 39.8 us; the launch traced here: 39.6 us
  Pallas kernels  37.8 us (95%)
  local copies, waits for them, and re-layouts  1.77 us (4%)
    pallas_call x1, Pallas kernels, on_device(): pl.pallas_call(functools.partial(kernel, plan), out_shape=jax.ShapeDtypeS...  37.8 us
    unnamed x1, local copies, waits for them, and re-layouts  1.77 us

profile of v1, /device:TPU:8, one launch (start us, length us, event | category | flops | bytes accessed | tf_op | source)
XLA Modules:
  0.0 39.6 jit_solution(1826369517822386386)
XLA Ops:
  0.0 37.8 %window.1 = f32[1,2,384,128]{3,2,1,0:T(8,128)} custom-call(f32[1,4,384,3072]{3,2,1,0:T(8,128)} %tensor_ref.1, f32[1,384,128]{2,1,0:T(8,128)} %panel_ref.1, f32[1,384,128]{2,1,0:T(8,128)} %fresh_ref.1, s32[1,2,128]{2,1,0:T(2,128)} %outcome_ref.1), custom_call_target="tpu_custom_call" | custom-call | tf_op jit(solution)/shard_map/window/pallas_call | solution.py:260
  37.8 1.8 %copy.6 = f32[1,2,384,128]{3,2,1,0:T(8,128)} copy(f32[1,2,384,128]{3,2,1,0:T(8,128)} %window.1) | data formatting | bytes 786432

commit v2 on v1

--- a/solution.py
+++ b/solution.py
@@ -9,6 +9,7 @@
 from jax.sharding import PartitionSpec as P
 
 TILE = 256
+LANES = 128
 
 
 def flipped(index, mask):
@@ -37,6 +38,11 @@
     core_in,
     stage_in,
     hop_in,
+    panel,
+    done,
+    panel_sem,
+    fresh_sem,
+    done_sem,
     load_sem,
     core_send,
     core_recv,
@@ -69,9 +75,16 @@
             load_sem.at[step * tiles + tile],
         )
 
+    panel_load = pltpu.make_async_copy(panel_ref.at[0], panel, panel_sem)
+    panel_load.start()
     for step in range(blocks):
         for tile in range(tiles):
             load(step, tile).start()
+    fresh_load = pltpu.make_async_copy(fresh_ref.at[0], hop_in, fresh_sem)
+
+    @pl.when(site == 0)
+    def _():
+        fresh_load.start()
 
     barrier = pltpu.get_barrier_semaphore()
     for bit in range(bits):
@@ -93,12 +106,25 @@
 
     def prepare(vectors, tick):
         chosen = outcome_ref[0, pl.ds(tick, 1), :]
-        for outcome in range(count):
-            stacked[pl.ds(outcome * rows, rows), :] = jnp.where(chosen == outcome, vectors, 0.0)
-        turned = stacked[...].T
-        upper = turned.astype(jnp.bfloat16)
-        left[pl.ds(0, samples), :] = upper
-        left[pl.ds(samples, samples), :] = (turned - upper.astype(jnp.float32)).astype(jnp.bfloat16)
+
+        def put(turned, start):
+            upper = turned.astype(jnp.bfloat16)
+            span = pl.ds(start, turned.shape[1])
+            left[pl.ds(0, samples), span] = upper
+            left[pl.ds(samples, samples), span] = (turned - upper.astype(jnp.float32)).astype(
+                jnp.bfloat16
+            )
+
+        if rows % LANES == 0:
+            whose = jnp.broadcast_to(chosen.astype(jnp.float32), (LANES, samples)).T
+            for first in range(0, rows, LANES):
+                turned = vectors[first : first + LANES].T
+                for outcome in range(count):
+                    put(jnp.where(whose == outcome, turned, 0.0), outcome * rows + first)
+        else:
+            for outcome in range(count):
+                stacked[pl.ds(outcome * rows, rows), :] = jnp.where(chosen == outcome, vectors, 0.0)
+            put(stacked[...].T, 0)
 
     def compute(tick, step):
         def one(tile):
@@ -165,12 +191,18 @@
 
     def hop_copy(side):
         return pltpu.make_async_remote_copy(
-            src_ref=out_ref.at[0, 0, pl.ds(side * half, half), :],
+            src_ref=done.at[0, pl.ds(side * half, half), :],
             dst_ref=hop_in.at[pl.ds(side * half, half), :],
             send_sem=hop_send.at[side],
             recv_sem=hop_recv.at[side],
             device_id={"site": site + 1},
             device_id_type=pl.DeviceIdType.MESH,
+        )
+
+    def store(tick, side):
+        span = pl.ds(side * half, half)
+        return pltpu.make_async_copy(
+            done.at[tick, span, :], out_ref.at[0, tick, span, :], done_sem.at[tick, side]
         )
 
     def settle(tick, upper):
@@ -185,13 +217,14 @@
                 stage_copy(tick, source, side).wait_recv()
                 total = total + stage_in[tick, source - 1, side]
             if bit is None:
-                out_ref[0, tick, pl.ds(side * half, half), :] = total
+                done[tick, pl.ds(side * half, half), :] = total
                 if tick == 0:
 
                     @pl.when(site < sites - 1)
                     def _():
                         hop_copy(side).start()
 
+                store(tick, side).start()
             else:
                 own[...] = total
                 stage_copy(tick, upper, side).start()
@@ -202,12 +235,13 @@
 
     for tick in range(ticks):
         if tick == 0:
-            prepare(panel_ref[0], 0)
+            panel_load.wait()
+            prepare(panel[...], 0)
         else:
 
             @pl.when(site == 0)
             def _():
-                hop_in[...] = fresh_ref[tick - 1]
+                fresh_load.wait()
 
             @pl.when(site > 0)
             def _():
@@ -237,6 +271,8 @@
             if upper:
                 for side in range(2):
                     stage_copy(tick, upper, side).wait_send()
+        for side in range(2):
+            store(tick, side).wait()
 
     @pl.when(site < sites - 1)
     def _():
@@ -260,9 +296,9 @@
     return pl.pallas_call(
         functools.partial(kernel, plan),
         out_shape=jax.ShapeDtypeStruct((1, ticks, chunk, samples), jnp.float32),
-        in_specs=[pl.BlockSpec(memory_space=pl.ANY)]
-        + [pl.BlockSpec(memory_space=pltpu.VMEM)] * 3,
-        out_specs=pl.BlockSpec(memory_space=pltpu.VMEM),
+        in_specs=[pl.BlockSpec(memory_space=pl.ANY)] * 3
+        + [pl.BlockSpec(memory_space=pltpu.VMEM)],
+        out_specs=pl.BlockSpec(memory_space=pl.ANY),
         scratch_shapes=[
             pltpu.VMEM((tiles, count, rows, TILE), jnp.float32),
             pltpu.VMEM((tiles, depth, TILE), jnp.bfloat16),
@@ -273,6 +309,11 @@
             pltpu.VMEM((ticks, uppers, chunk, samples), jnp.float32),
             pltpu.VMEM((ticks, uppers - 1, 2, half, samples), jnp.float32),
             pltpu.VMEM((chunk, samples), jnp.float32),
+            pltpu.VMEM((rows, samples), jnp.float32),
+            pltpu.VMEM((ticks, chunk, samples), jnp.float32),
+            dma,
+            dma,
+            dma((ticks, 2)),
             dma((tiles,)),
             dma((ticks, uppers)),
             dma((ticks, uppers)),

time: 39.8 us -> 44.8 us (1.13)
  Pallas kernels: 37.8 us -> 42.9 us
    pallas_call x1, Pallas kernels: 37.8 us -> 42.9 us  [on_device(): pl.pallas_call(functools.partial(kernel, plan), out_shape=jax.ShapeDtypeS...]
where the time goes in v2:
time: 44.8 us; the launch traced here: 44.7 us
  Pallas kernels  42.9 us (96%)
  local copies, waits for them, and re-layouts  1.77 us (4%)
    pallas_call x1, Pallas kernels, on_device(): pl.pallas_call(functools.partial(kernel, plan), out_shape=jax.ShapeDtypeS...  42.9 us
    unnamed x1, local copies, waits for them, and re-layouts  1.77 us

profile of v2, /device:TPU:8, one launch (start us, length us, event | category | flops | bytes accessed | tf_op | source)
XLA Modules:
  0.0 44.7 jit_solution(16361860221400386272)
XLA Ops:
  0.0 42.9 %window.1 = f32[1,2,384,128]{3,2,1,0:T(8,128)} custom-call(f32[1,4,384,3072]{3,2,1,0:T(8,128)} %tensor_ref.1, f32[1,384,128]{2,1,0:T(8,128)} %panel_ref.1, f32[1,384,128]{2,1,0:T(8,128)} %fresh_ref.1, s32[1,2,128]{2,1,0:T(2,128)} %outcome_ref.1), custom_call_target="tpu_custom_call" | custom-call | tf_op jit(solution)/shard_map/window/pallas_call | solution.py:296
  42.9 1.8 %copy.6 = f32[1,2,384,128]{3,2,1,0:T(8,128)} copy(f32[1,2,384,128]{3,2,1,0:T(8,128)} %window.1) | data formatting | bytes 786432

commit v3 on v0

v3 whole, which is shorter than its diff:
```python
import functools
import math

import jax
import jax.numpy as jnp
from jax import lax
from jax.experimental import pallas as pl
from jax.experimental.pallas import tpu as pltpu
from jax.sharding import PartitionSpec as P

TILE = 256
LANES = 128


def flipped(index, mask):
    result = index
    bit = 0
    while (1 << bit) <= mask:
        if mask >> bit & 1:
            result = result + (1 - 2 * ((index // (1 << bit)) % 2)) * (1 << bit)
        bit += 1
    return result


CORE_LAG = 1
LINK_LAG = 2


class Layout:
    def __init__(self, bond, columns):
        self.chunk = columns // bond
        self.tiles = columns // TILE
        self.uppers = bond // 2
        self.bits = bond.bit_length() - 1
        if self.chunk % LANES == 0:
            self.pieces, self.per_block = self.chunk // LANES, 2
            self.size = LANES
            self.split()
            pairs = [(upper, piece) for upper in range(self.uppers) for piece in range(self.pieces)]
            self.items = [[pair] for pair in sorted(pairs, key=self.rank)]
            self.group = self.pieces
        else:
            self.pieces, self.size = 1, self.chunk
            self.split()
            width = math.lcm(TILE, 2 * self.chunk)
            self.per_block = width // self.chunk
            self.group = self.block_tiles = width // TILE
            group = self.per_block // 2
            self.items = []
            for block in reversed(range(bond // self.per_block)):
                self.items += [[] for _ in range(self.block_tiles - 1)]
                self.items.append(
                    [(block * group + inner, 0) for inner in reversed(range(group))]
                )
        self.when = {item: tile for tile, items in enumerate(self.items) for item in items}

    def split(self):
        self.strands = []
        for piece in range(self.pieces):
            if 2 * piece + 1 == self.pieces:
                half = self.size // 2
                self.strands += [(piece, 0, half, False), (piece, half, half, True)]
            else:
                self.strands.append((piece, 0, self.size, 2 * piece >= self.pieces))

    def rank(self, pair):
        upper, piece = pair
        strands = self.strands_of(piece)
        late = sum(len(self.path(upper, strand)[0]) for strand in strands) / len(strands)
        middle = -abs(2 * piece + 1 - self.pieces)
        return -upper.bit_count(), late, middle, upper, piece

    def column(self, me, tile, part):
        if self.chunk % LANES == 0:
            ((upper, piece),) = self.items[tile]
            return (2 * flipped(me // 2, upper) + part) * self.chunk + piece * LANES
        step = tile // self.block_tiles
        block = flipped(me // self.per_block, self.tiles // self.block_tiles - 1 - step)
        width = self.block_tiles * TILE
        return block * width + tile % self.block_tiles * TILE + part * LANES

    def row(self, me, rel, piece):
        offset = flipped(me % self.per_block, rel % self.per_block) * self.size
        tile = self.when[rel // 2, piece]
        if self.chunk % LANES == 0:
            return tile * TILE + offset
        return tile // self.block_tiles * self.block_tiles * TILE + offset

    def path(self, upper, strand):
        order = list(range(1, self.bits))
        if self.strands[strand][3]:
            order.reverse()
        earlier = []
        for bit in order:
            if upper >> (bit - 1) & 1:
                return earlier, bit
            earlier.append(bit)
        return earlier, None

    def strands_of(self, piece):
        return [strand for strand, entry in enumerate(self.strands) if entry[0] == piece]

    def events(self):
        found, sent = [], {}
        for tile, items in enumerate(self.items):
            for upper, piece in items:
                pair = (tile // self.group + CORE_LAG, 0)
                found.append((pair, 0, upper, piece, None))
                for strand in self.strands_of(piece):
                    earlier, _ = self.path(upper, strand)
                    moment = pair
                    for bit in earlier:
                        source = sent[upper | 1 << (bit - 1), strand]
                        moment = max(moment, (source[0] + LINK_LAG, 1))
                    sent[upper, strand] = moment
                    if earlier:
                        found.append((moment, 1, upper, piece, strand))
        return sorted(found, key=lambda event: event[:2])


def kernel(
    plan,
    tensor_ref,
    panel_ref,
    fresh_ref,
    outcome_ref,
    out_ref,
    raw,
    high,
    low,
    stacked,
    left,
    part,
    core_in,
    stage_in,
    hop_in,
    load_sem,
    core_send,
    core_recv,
    stage_send,
    stage_recv,
    hop_send,
    hop_recv,
):
    layout, sites, ticks, count, rows, samples = plan
    me = lax.axis_index("bond")
    site = lax.axis_index("site")
    mesh_id = pl.DeviceIdType.MESH

    def at(mask):
        return {"bond": flipped(me, mask)}

    def load(tile, side):
        column = pl.multiple_of(layout.column(me, tile, side), LANES)
        return pltpu.make_async_copy(
            tensor_ref.at[0, :, :, pl.ds(column, LANES)],
            raw.at[tile, :, :, pl.ds(side * LANES, LANES)],
            load_sem.at[tile, side],
        )

    for tile in range(layout.tiles):
        for side in range(2):
            load(tile, side).start()
    barrier = pltpu.get_barrier_semaphore()
    for bit in range(layout.bits):
        pl.semaphore_signal(barrier, inc=1, device_id=at(1 << bit), device_id_type=mesh_id)

    @pl.when(site > 0)
    def _():
        pl.semaphore_signal(barrier, inc=1, device_id={"site": site - 1}, device_id_type=mesh_id)

    @pl.when(site < sites - 1)
    def _():
        pl.semaphore_signal(barrier, inc=1, device_id={"site": site + 1}, device_id_type=mesh_id)

    def greet():
        edges = (site > 0).astype(jnp.int32) + (site < sites - 1).astype(jnp.int32)
        pl.semaphore_wait(barrier, layout.bits + edges)

    def put(turned, start, size):
        upper = turned.astype(jnp.bfloat16)
        left[pl.ds(0, samples), pl.ds(start, size)] = upper
        left[pl.ds(samples, samples), pl.ds(start, size)] = (
            turned - upper.astype(jnp.float32)
        ).astype(jnp.bfloat16)

    def prepare(vectors, tick, piece):
        chosen = outcome_ref[0, pl.ds(tick, 1), :]
        if layout.size % LANES == 0:
            turned = vectors.T
            whose = jnp.broadcast_to(chosen.astype(jnp.float32), (LANES, samples)).T
            for outcome in range(count):
                start = outcome * rows + piece * LANES
                put(jnp.where(whose == outcome, turned, 0.0), start, LANES)
        else:
            for outcome in range(count):
                stacked[pl.ds(outcome * rows, rows), :] = jnp.where(chosen == outcome, vectors, 0.0)
            put(stacked[...].T, 0, count * rows)

    def compute(tick, tile):
        if tick == 0:
            for outcome in range(count):
                values = raw[tile, outcome]
                upper = values.astype(jnp.bfloat16)
                high[tile, pl.ds(outcome * rows, rows), :] = upper
                low[tile, pl.ds(outcome * rows, rows), :] = (
                    values - upper.astype(jnp.float32)
                ).astype(jnp.bfloat16)
        both = jnp.dot(left[...], high[tile], preferred_element_type=jnp.float32)
        rest = jnp.dot(left[pl.ds(0, samples), :], low[tile], preferred_element_type=jnp.float32)
        total = both[:samples] + (both[samples:] + rest)
        part[tick, pl.ds(tile * TILE, TILE), :] = total.T

    def rows_of(tick, rel, piece, start, size):
        row = pl.multiple_of(layout.row(me, rel, piece) + start, 8)
        return part.at[tick, pl.ds(row, size), :]

    def core_copy(tick, upper, piece):
        return pltpu.make_async_remote_copy(
            src_ref=rows_of(tick, 2 * upper + 1, piece, 0, layout.size),
            dst_ref=core_in.at[tick, upper, piece],
            send_sem=core_send.at[tick, upper, piece],
            recv_sem=core_recv.at[tick, upper, piece],
            device_id=at(1),
            device_id_type=mesh_id,
        )

    def stage_copy(tick, upper, strand):
        piece, start, size, _ = layout.strands[strand]
        _, bit = layout.path(upper, strand)
        return pltpu.make_async_remote_copy(
            src_ref=rows_of(tick, 2 * upper, piece, start, size),
            dst_ref=stage_in.at[tick, upper - 1, pl.ds(piece * layout.size + start, size), :],
            send_sem=stage_send.at[tick, upper - 1, strand],
            recv_sem=stage_recv.at[tick, upper - 1, strand],
            device_id=at(1 << bit),
            device_id_type=mesh_id,
        )

    def span_of(strand):
        piece, start, size, _ = layout.strands[strand]
        return pl.ds(piece * layout.size + start, size)

    def hop_copy(tick, strand):
        return pltpu.make_async_remote_copy(
            src_ref=out_ref.at[0, tick, span_of(strand), :],
            dst_ref=hop_in.at[tick, span_of(strand), :],
            send_sem=hop_send.at[tick, strand],
            recv_sem=hop_recv.at[tick, strand],
            device_id={"site": site + 1},
            device_id_type=mesh_id,
        )

    def settle(tick, event):
        _, kind, upper, piece, strand = event
        if kind == 0:
            core_copy(tick, upper, piece).wait_recv()
            own = rows_of(tick, 2 * upper, piece, 0, layout.size)
            own[...] += core_in[tick, upper, piece]
            for strand in layout.strands_of(piece):
                if upper and not layout.path(upper, strand)[0]:
                    stage_copy(tick, upper, strand).start()
            return
        earlier, bit = layout.path(upper, strand)
        _, start, size, _ = layout.strands[strand]
        own = rows_of(tick, 2 * upper, piece, start, size)
        total = own[...]
        for before in earlier:
            source = upper | 1 << (before - 1)
            stage_copy(tick, source, strand).wait_recv()
            total = total + stage_in[tick, source - 1, span_of(strand), :]
        if bit is not None:
            own[...] = total
            stage_copy(tick, upper, strand).start()
            return
        out_ref[0, tick, span_of(strand), :] = total
        if tick + 1 < ticks:

            @pl.when(site < sites - 1)
            def _():
                hop_copy(tick, strand).start()

    for tick in range(ticks):
        for piece in range(layout.pieces):
            span = pl.ds(piece * layout.size, layout.size)
            if tick == 0:
                prepare(panel_ref[0, span, :], tick, piece)
                continue

            @pl.when(site == 0)
            def _():
                hop_in[tick - 1, span, :] = fresh_ref[tick - 1, span, :]

            @pl.when(site > 0)
            def _():
                for strand in layout.strands_of(piece):
                    hop_copy(tick - 1, strand).wait_recv()

            prepare(hop_in[tick - 1, span, :], tick, piece)
        pending = layout.events()
        for first in range(0, layout.tiles, layout.group):
            members = range(first, first + layout.group)
            if tick == 0:
                for tile in members:
                    for side in range(2):
                        load(tile, side).wait()
            for tile in members:
                compute(tick, tile)
            if tick == 0 and first == 0:
                greet()
            for tile in members:
                for upper, piece in layout.items[tile]:
                    core_copy(tick, upper, piece).start()
            while pending and pending[0][0][0] <= first // layout.group:
                settle(tick, pending.pop(0))
        for event in pending:
            settle(tick, event)

    strands = range(len(layout.strands))
    for tick in range(ticks):
        for upper in range(layout.uppers):
            for piece in range(layout.pieces):
                core_copy(tick, upper, piece).wait_send()
            if upper:
                for strand in strands:
                    stage_copy(tick, upper, strand).wait_send()

    @pl.when(site < sites - 1)
    def _():
        for tick in range(ticks - 1):
            for strand in strands:
                hop_copy(tick, strand).wait_send()


def on_device(sites, bond, site_tensor, panels, fresh, outcomes):
    _, count, rows, columns = site_tensor.shape
    samples = panels.shape[2]
    ticks = outcomes.shape[1]
    layout = Layout(bond, columns)
    tiles, uppers, pieces = layout.tiles, layout.uppers, layout.pieces
    chunk, size, strands = layout.chunk, layout.size, len(layout.strands)
    depth = count * rows
    dma = pltpu.SemaphoreType.DMA
    return pl.pallas_call(
        functools.partial(kernel, (layout, sites, ticks, count, rows, samples)),
        out_shape=jax.ShapeDtypeStruct((1, ticks, chunk, samples), jnp.float32),
        in_specs=[pl.BlockSpec(memory_space=pl.ANY)]
        + [pl.BlockSpec(memory_space=pltpu.VMEM)] * 3,
        out_specs=pl.BlockSpec(memory_space=pltpu.VMEM),
        scratch_shapes=[
            pltpu.VMEM((tiles, count, rows, TILE), jnp.float32),
            pltpu.VMEM((tiles, depth, TILE), jnp.bfloat16),
            pltpu.VMEM((tiles, depth, TILE), jnp.bfloat16),
            pltpu.VMEM((depth, samples), jnp.float32),
            pltpu.VMEM((2 * samples, depth), jnp.bfloat16),
            pltpu.VMEM((ticks, columns, samples), jnp.float32),
            pltpu.VMEM((ticks, uppers, pieces, size, samples), jnp.float32),
            pltpu.VMEM((ticks, uppers - 1, chunk, samples), jnp.float32),
            pltpu.VMEM((ticks - 1, chunk, samples), jnp.float32),
            dma((tiles, 2)),
            dma((ticks, uppers, pieces)),
            dma((ticks, uppers, pieces)),
            dma((ticks, uppers - 1, strands)),
            dma((ticks, uppers - 1, strands)),
            dma((ticks - 1, strands)),
            dma((ticks - 1, strands)),
        ],
        compiler_params=pltpu.CompilerParams(
            collective_id=0, has_side_effects=True, vmem_limit_bytes=60 * 1024 * 1024
        ),
        name="window",
    )(site_tensor, panels, fresh, outcomes)


def solution(mesh):
    placed = (
        P("site", None, "bond", None),
        P("site", "bond", None),
        P(None, "bond", None),
        P("site", None, None),
    )
    return jax.shard_map(
        functools.partial(on_device, mesh.shape["site"], mesh.shape["bond"]),
        mesh=mesh,
        in_specs=placed,
        out_specs=P("site", None, "bond", None),
        check_vma=False,
    )
```

time: 157 us -> 35.7 us (0.23)
  waiting for transfers between devices: 83 us -> 0 us
  matrix products: 51.3 us -> 0 us
  Pallas kernels: 0 us -> 33.8 us
  between operations: 13.4 us -> 0.01 us
  starting transfers between devices: 3.62 us -> 0 us
  other arithmetic: 1.71 us -> 0 us
    reduce_scatter x2 -> x0, waiting for transfers between devices: 78 us -> none  [advance(): lax.psum_scatter(contribute(tensor, vectors, selected), 'bond', scatter_d...]
    dot_general x2 -> x0, matrix products: 51.3 us -> none  [contribute(): lax.dot_general(tensor, vectors, (((1,), (0,)), ((), ())), precision=lax....]
    pallas_call x0 -> x1, Pallas kernels: none -> 33.8 us  [on_device(): pl.pallas_call(functools.partial(kernel, (layout, sites, ticks, count, ro...]
    ppermute x1 -> x0, waiting for transfers between devices: 4.94 us -> none  [from_behind(): lax.ppermute(value, axis, [(source, source + steps) for source in range(i...]
    ppermute x1 -> x0, starting transfers between devices: 3.57 us -> none  [from_behind(): lax.ppermute(value, axis, [(source, source + steps) for source in range(i...]
    broadcast_in_dim x1 -> x0, other arithmetic: 1.7 us -> none  [on_device(): return jnp.stack(results, 0)[None]]
    reduce_sum x1 -> x0, local copies, waits for them, and re-layouts: 1.63 us -> none  [contribute(): return jnp.sum(products * chosen[:, None, :], axis=0)]
  transfers between devices with their start and end apart: 3 -> 0, of which waited for: 3 -> 0; matrix products, arithmetic and copies ran while one was open for 0% -> 0% of each run, Pallas kernels for 0% -> 0%
where the time goes in v3:
time: 35.7 us; the launch traced here: 35.5 us
  Pallas kernels  33.8 us (95%)
  local copies, waits for them, and re-layouts  1.77 us (5%)
    pallas_call x1, Pallas kernels, on_device(): pl.pallas_call(functools.partial(kernel, (layout, sites, ticks, count, ro...  33.8 us
    unnamed x1, local copies, waits for them, and re-layouts  1.77 us

profile of v3, /device:TPU:8, one launch (start us, length us, event | category | flops | bytes accessed | tf_op | source)
XLA Modules:
  0.0 35.5 jit_solution(10762397853264378639)
XLA Ops:
  0.0 33.8 %window.1 = f32[1,2,384,128]{3,2,1,0:T(8,128)} custom-call(f32[1,4,384,3072]{3,2,1,0:T(8,128)} %tensor_ref.1, f32[1,384,128]{2,1,0:T(8,128)} %panel_ref.1, f32[1,384,128]{2,1,0:T(8,128)} %fresh_ref.1, s32[1,2,128]{2,1,0:T(2,128)} %outcome_ref.1), custom_call_target="tpu_custom_call" | custom-call | tf_op jit(solution)/shard_map/window/pallas_call | solution.py:344
  33.8 1.8 %copy.6 = f32[1,2,384,128]{3,2,1,0:T(8,128)} copy(f32[1,2,384,128]{3,2,1,0:T(8,128)} %window.1) | data formatting | bytes 786432
